TPU v7x, 32 devices: a whole 2x2x4 slice. The times are simulated.
32 devices in a mesh: aux: 2 (over x), pair: 16 (over z, y, core).
Axes of the slice: x: 2, y: 2, z: 4, core: 2. Of those that a mesh axis runs over, the one named last changes fastest.
Arguments:
- three_index: bfloat16 [256, 256, 2048], P('pair', None, 'aux'), may hold values from -0.875 to 0.875
- fock_diag: float32 [256], replicated, may hold values from -1.2 to -0.3
- pair_occ: int32 [496, 2], P('pair'), may hold values from 0 to 255, as said below
- pno_count: int32 [496], P('pair'), may hold values from 32 to 128
- pno_energy: float32 [496, 128], P('pair'), may hold values from 0.3 to 3
- pno_coef: bfloat16 [496, 2, 256, 128], P('pair'), may hold values from -0.375 to 0.375
Outputs:
- pair_energy: float32 [496], P('pair')
- grad_ints: float32 [256, 256, 2048], P('pair', None, 'aux')
Inputs may be any that keep to these rules, and one draw needn't show every extreme that they name: `pair_occ`: orbital o belongs to the block o // 16. Among the 62 orbitals named by the pairs of one aligned block of 31 rows, at most 4 belong to any one orbital block, and one orbital block receives exactly 4 from every such row block; i may equal j.
All inputs are finite; a program needn't handle non-finite values.
Results may differ from a plain program's by a relative error of at most 0.0061.
Values may be sent and summed in bfloat16 or wider, within the bound.
No kernel may reach another device: no remote copies, remote signals or barrier semaphores. Data moves between devices by JAX's collectives and lax.ppermute only.
A program may use at most 128 MiB of HBM per device.

v0:
```python
import jax
import jax.numpy as jnp
from jax import lax
from jax.sharding import PartitionSpec as P


def local(three_index, fock_diag, pair_occ, pno_count, pno_energy, pno_coef):
    groups = lax.axis_size("pair")
    occ_dev = three_index.shape[0]
    width_dom = three_index.shape[1]
    width_aux = three_index.shape[2]
    pair_dev = pair_occ.shape[0]
    width_pno = pno_coef.shape[3]
    halves = 2 * pair_dev
    capacity = max(2, halves // groups + 1)
    slots = groups * capacity
    occ_flat = pair_occ.reshape(halves)
    owner_of = occ_flat // occ_dev
    local_index = occ_flat % occ_dev
    owner_hot = (owner_of[:, None] == jnp.arange(groups, dtype=jnp.int32)[None, :]).astype(
        jnp.int32
    )
    before = jnp.cumsum(owner_hot, axis=0) - owner_hot
    rank_in = jnp.sum(before * owner_hot, axis=1)
    slot_of = owner_of * capacity + rank_in
    request = jnp.zeros((slots,), jnp.int32).at[slot_of].set(local_index + 1)
    arrived = lax.all_to_all(
        request.reshape(groups, capacity), "pair", split_axis=0, concat_axis=0, tiled=True
    ).reshape(slots)
    is_live = arrived > 0
    row_index = jnp.maximum(arrived - 1, 0)
    selected = jnp.take(three_index, row_index, axis=0)
    selected = jnp.where(is_live[:, None, None], selected, jnp.zeros_like(selected))
    coef_half = pno_coef.reshape(halves, width_dom, width_pno)
    coef_send = jnp.zeros((slots, width_dom, width_pno), jnp.bfloat16).at[slot_of].set(coef_half)
    coef_recv = lax.all_to_all(
        coef_send.reshape(groups, capacity, width_dom, width_pno),
        "pair",
        split_axis=0,
        concat_axis=0,
        tiled=True,
    )
    coef_recv = coef_recv.reshape(slots, width_dom, width_pno)
    proj_here = jnp.einsum(
        "sdp,sdq->spq", coef_recv, selected, preferred_element_type=jnp.float32
    ).astype(jnp.bfloat16)
    proj_back = lax.all_to_all(
        proj_here.reshape(groups, capacity, width_pno, width_aux),
        "pair",
        split_axis=0,
        concat_axis=0,
        tiled=True,
    )
    projected = jnp.take(proj_back.reshape(slots, width_pno, width_aux), slot_of, axis=0)
    paired = projected.reshape(pair_dev, 2, width_pno, width_aux)
    rows_i = paired[:, 0]
    rows_j = paired[:, 1]
    partial_sum = jnp.einsum("kpq,krq->kpr", rows_i, rows_j, preferred_element_type=jnp.float32)
    coupling = lax.psum(partial_sum, "aux")
    fock_i = jnp.take(fock_diag, pair_occ[:, 0])
    fock_j = jnp.take(fock_diag, pair_occ[:, 1])
    denom = pno_energy[:, :, None] + pno_energy[:, None, :] - (fock_i + fock_j)[:, None, None]
    in_pno = jnp.arange(width_pno, dtype=jnp.int32)[None, :] < pno_count[:, None]
    both_in = in_pno[:, :, None] & in_pno[:, None, :]
    amplitude = jnp.where(both_in, -coupling / denom, jnp.float32(0.0))
    mixed = 2.0 * amplitude - jnp.swapaxes(amplitude, 1, 2)
    energy = jnp.sum(coupling * mixed, axis=(1, 2)) / (width_pno * width_pno)
    weights = mixed.astype(jnp.bfloat16)
    gamma_i = jnp.einsum(
        "kab,kbq->kaq", weights, rows_j, preferred_element_type=jnp.float32
    ).astype(jnp.bfloat16)
    gamma_j = jnp.einsum(
        "kba,kbq->kaq", weights, rows_i, preferred_element_type=jnp.float32
    ).astype(jnp.bfloat16)
    gamma = jnp.stack([gamma_i, gamma_j], axis=1).reshape(halves, width_pno, width_aux)
    gamma_send = jnp.zeros((slots, width_pno, width_aux), jnp.bfloat16).at[slot_of].set(gamma)
    gamma_recv = lax.all_to_all(
        gamma_send.reshape(groups, capacity, width_pno, width_aux),
        "pair",
        split_axis=0,
        concat_axis=0,
        tiled=True,
    )
    gamma_recv = gamma_recv.reshape(slots, width_pno, width_aux)
    terms = jnp.einsum(
        "sdp,spq->sdq", coef_recv, gamma_recv, preferred_element_type=jnp.float32
    ).astype(jnp.bfloat16)
    occ_hot = (row_index[None, :] == jnp.arange(occ_dev, dtype=jnp.int32)[:, None]) & is_live[
        None, :
    ]
    grad = jnp.dot(
        occ_hot.astype(jnp.bfloat16),
        terms.reshape(slots, width_dom * width_aux),
        preferred_element_type=jnp.float32,
    )
    return (energy, grad.reshape(occ_dev, width_dom, width_aux))


def solution(mesh):
    placed = (
        P("pair", None, "aux"),
        P(),
        P("pair", None),
        P("pair"),
        P("pair", None),
        P("pair", None, None, None),
    )
    return jax.shard_map(
        local,
        mesh=mesh,
        in_specs=placed,
        out_specs=(P("pair"), P("pair", None, "aux")),
        check_vma=False,
    )
```

profile of v0, /device:TPU:13, one launch (start us, length us, event | category | flops | bytes accessed | tf_op | source)
XLA Modules:
  0.0 1180.7 jit_solution(13151449799421802586)
XLA Ops:
  7.2 0.8 copy.53
  8.6 0.8 scatter_custom_fusion.1
  10.0 6.5 all-to-all-start.1
  16.5 3.0 broadcast_in_dim.61
  19.6 11.7 scatter_fusion
  31.3 6.4 copy.56
  37.7 6.0 all-to-all-start
  44.0 15.7 %gather_fusion = bf16[64,256,1024]{2,1,0:T(8,128)(2,1)} fusion(bf16[16,256,1024]{2,1,0:T(8,128)(2,1)} %param.8, s32[1024]{0:T(1024)S(1)} %pad_clamp_fusion.3), kind=kCustom, calls=%fused_computation.2 | custom fusion | bytes 67109120 | tf_op jit(solution)/shard_map/jit(_take)/gather | solution.py:32
  59.7 76.5 %all-to-all-done = bf16[16,4,256,128]{2,3,1,0:T(8,128)(2,1)} async-done(((bf16[16,4,256,128]{2,3,1,0:T(8,128)(2,1)}), bf16[16,4,256,128]{2,3,1,0:T(8,128)(2,1)}, u32[]{:S(2)}, u32[]{:S(2)}) %all-to-all-start) | async-done | bytes 4194336 | tf_op jit(solution)/shard_map/all_to_all | solution.py:36
  136.2 18.3 %fusion.10 = bf16[64,128,1024]{2,1,0:T(8,128)(2,1)} fusion(bf16[64,256,128]{1,2,0:T(8,128)(2,1)} %bitcast.4, bf16[64,256,1024]{2,1,0:T(8,128)(2,1)} %gather_fusion, pred[64]{0:T(512)(128)(4,1)S(1)} %broadcast_compare_fusion, pred[64]{0:T(512)(128)(4,1)S(1)} %gt.15), kind=kOutput, calls=%fused_computation.20 | convolution fusion | flops 4336910336 | bytes 54526080 | tf_op jit(solution)/shard_map/sdp,sdq->spq/dot_general | solution.py:44
  154.5 5.2 all-to-all-start.2
  160.1 361.4 %all-to-all-done.2 = bf16[16,4,128,1024]{3,2,1,0:T(8,128)(2,1)} async-done(((bf16[16,4,128,1024]{3,2,1,0:T(8,128)(2,1)}), bf16[16,4,128,1024]{3,2,1,0:T(8,128)(2,1)}, u32[]{:S(2)}, u32[]{:S(2)}) %all-to-all-start.2) | async-done | bytes 16777248 | tf_op jit(solution)/shard_map/all_to_all | solution.py:47
  521.5 13.3 %gather_fusion.1 = bf16[62,128,1024]{2,1,0:T(8,128)(2,1)} fusion(bf16[64,128,1024]{2,1,0:T(8,128)(2,1)} %bitcast.7, s32[1024]{0:T(1024)S(1)} %pad_clamp_fusion.2), kind=kCustom, calls=%fused_computation.3 | custom fusion | bytes 32506104 | tf_op jit(solution)/shard_map/jit(_take)/gather | solution.py:54
  534.8 13.8 %copy_select_fusion = bf16[31,2,128,1024]{3,2,0,1:T(8,128)(2,1)} fusion(bf16[31,2,128,1024]{3,2,1,0:T(8,128)(2,1)} %bitcast.68, pred[31,2]{0,1:T(4,128)(4,1)S(1)} %compare_and_fusion), kind=kLoop, calls=%fused_computation.19 | loop fusion | flops 8126464 | bytes 32505918 | tf_op jit(solution)/shard_map/jit(_take)/select_n | solution.py:54
  548.7 9.2 fusion.14
  558.0 0.7 gather_fusion.2
  559.5 59.4 %all-reduce.2.cloned.1.call-done = f32[31,128,128]{2,1,0:T(8,128)} async-done(((f32[31,128,128]{2,1,0:T(8,128)}), f32[31,128,128]{2,1,0:T(8,128)}) %all-reduce.2.cloned.1.call-update) | async-done | bytes 2031632 | tf_op jit(solution)/shard_map/psum | solution.py:59
  618.9 2.3 copy.59
  621.2 2.6 broadcast_multiply_fusion
  623.9 2.9 copy.60
  626.7 3.8 fusion.16
  630.5 5.6 convert_bitcast_fusion.1
  636.1 8.9 convert_bitcast_fusion
  645.0 6.2 pad_maximum_fusion
  651.2 6.4 copy.62
  657.6 6.1 broadcast_in_dim.68
  663.7 41.4 %scatter_fusion.1 = bf16[64,128,1024]{2,1,0:T(8,128)(2,1)} fusion(bf16[64,128,1024]{2,1,0:T(8,128)(2,1)} %broadcast_in_dim.68, s32[62]{0:T(128)S(1)} %fusion.25, bf16[62,128,1024]{2,1,0:T(8,128)(2,1)} %bitcast.67), kind=kCustom, calls=%fused_computation.6 | custom fusion | bytes 48759032 | tf_op jit(solution)/shard_map/scatter | solution.py:76
  705.1 6.5 all-to-all-start.3
  712.1 361.6 %all-to-all-done.3 = bf16[16,4,128,1024]{3,2,1,0:T(8,128)(2,1)} async-done(((bf16[16,4,128,1024]{3,2,1,0:T(8,128)(2,1)}), bf16[16,4,128,1024]{3,2,1,0:T(8,128)(2,1)}, u32[]{:S(2)}, u32[]{:S(2)}) %all-to-all-start.3) | async-done | bytes 16777248 | tf_op jit(solution)/shard_map/all_to_all | solution.py:77
  1073.7 21.3 %convolution_convert_fusion = bf16[64,256,1024]{2,1,0:T(8,128)(2,1)} fusion(bf16[64,256,128]{1,2,0:T(8,128)(2,1)} %bitcast.4, bf16[64,128,1024]{2,1,0:T(8,128)(2,1)} %bitcast.19), kind=kOutput, calls=%fused_computation.15 | convolution fusion | flops 4311744512 | bytes 54525952 | tf_op jit(solution)/shard_map/sdp,spq->sdq/dot_general | solution.py:85
  1095.0 60.6 %fusion = f32[16,256,1024]{2,0,1:T(8,128)} fusion(s32[64]{0:T(128)S(1)} %max.23, pred[64]{0:T(512)(128)(4,1)S(1)} %gt.15, bf16[8,8,256,1024]{3,2,1,0:T(8,128)(2,1)} %bitcast.65), kind=kOutput, calls=%fused_computation.7 | convolution fusion | flops 536872960 | bytes 50331968 | tf_op jit(solution)/shard_map/dot_general | solution.py:91
  1155.6 17.8 %copy.65 = f32[16,256,1024]{2,1,0:T(8,128)} copy(f32[16,256,1024]{2,0,1:T(8,128)} %fusion) | data formatting | bytes 33554432
  (37 shorter events, 3.3 us)
Async XLA Ops:
  7.2 550.8 %copy-start = (f32[256]{0:T(256)S(1)}, f32[256]{0:T(256)}, u32[]{:S(2)}) copy-start(f32[256]{0:T(256)} %param.9) | copy-start | bytes 3076
  10.0 27.7 %all-to-all-start.1 = ((s32[16,1,4]{2,1,0:T(1,128)}), s32[16,1,4]{2,1,0:T(1,128)S(1)}, u32[]{:S(2)}, u32[]{:S(2)}) async-start(s32[16,1,4]{2,1,0:T(1,128)} %bitcast.5), calls=%async_computation.1 | async-start | bytes 16384 | tf_op jit(solution)/shard_map/all_to_all | solution.py:27
  37.7 98.5 %all-to-all-start = ((bf16[16,4,256,128]{2,3,1,0:T(8,128)(2,1)}), bf16[16,4,256,128]{2,3,1,0:T(8,128)(2,1)}, u32[]{:S(2)}, u32[]{:S(2)}) async-start(bf16[16,4,256,128]{2,3,1,0:T(8,128)(2,1)} %copy.56), calls=%async_computation | async-start | bytes 8388608 | tf_op jit(solution)/shard_map/all_to_all | solution.py:36
  154.5 5.6 copy-start.3
  154.5 367.0 %all-to-all-start.2 = ((bf16[16,4,128,1024]{3,2,1,0:T(8,128)(2,1)}), bf16[16,4,128,1024]{3,2,1,0:T(8,128)(2,1)}, u32[]{:S(2)}, u32[]{:S(2)}) async-start(bf16[16,4,128,1024]{3,2,1,0:T(8,128)(2,1)} %bitcast.70), calls=%async_computation.2 | async-start | bytes 33554432 | tf_op jit(solution)/shard_map/all_to_all | solution.py:47
  159.6 459.2 %all-reduce.2.cloned.1.call-start = ((), (), s32[]{:S(2)}) async-start(), calls=%async_computation.4 | async-start | bytes 4063232 | tf_op jit(solution)/shard_map/psum | solution.py:59
  548.7 10.7 copy-start.4
  548.7 72.5 %copy-start.2 = (f32[31,128]{1,0:T(8,128)S(1)}, f32[31,128]{1,0:T(8,128)}, u32[]{:S(2)}) copy-start(f32[31,128]{1,0:T(8,128)} %param.12) | copy-start | bytes 47620
  705.1 368.6 %all-to-all-start.3 = ((bf16[16,4,128,1024]{3,2,1,0:T(8,128)(2,1)}), bf16[16,4,128,1024]{3,2,1,0:T(8,128)(2,1)}, u32[]{:S(2)}, u32[]{:S(2)}) async-start(bf16[16,4,128,1024]{3,2,1,0:T(8,128)(2,1)} %bitcast.66), calls=%async_computation.3 | async-start | bytes 33554432 | tf_op jit(solution)/shard_map/all_to_all | solution.py:77
  1095.0 78.3 %copy-start.1 = (f32[256]{0:T(256)S(1)}, f32[256]{0:T(256)}, u32[]{:S(2)}) copy-start(f32[256]{0:T(256)} %param.9) | copy-start | bytes 3076
Sparse Core Ops, SparseCore 0:
  558.1 60.7 all-reduce.1
where the time goes:
time: 1190 us; the launch traced here: 1180 us
  waiting for transfers between devices  859 us (72%)
  local copies, waits for them, and re-layouts  131 us (11%)
  matrix products  124 us (10%)
  other arithmetic  27.5 us (2%)
  starting transfers between devices  24.4 us (2%)
  between operations  14.6 us (1%)
    all_to_all x1, waiting for transfers between devices, local(): lax.all_to_all(gamma_send.reshape(groups, capacity, width_pno, width_aux)...  362 us
    all_to_all x1, waiting for transfers between devices, local(): lax.all_to_all(proj_here.reshape(groups, capacity, width_pno, width_aux),...  361 us
    all_to_all x1, waiting for transfers between devices, local(): lax.all_to_all(coef_send.reshape(groups, capacity, width_dom, width_pno),...  76.5 us
    dot_general x1, matrix products, local(): jnp.dot(occ_hot.astype(jnp.bfloat16), terms.reshape(slots, width_dom * wi...  60.6 us
    psum x1, waiting for transfers between devices, local(): coupling = lax.psum(partial_sum, 'aux')  59.4 us
    scatter x1, local copies, waits for them, and re-layouts, local(): jnp.zeros((slots, width_pno, width_aux), jnp.bfloat16).at[slot_of]  41.4 us
  transfers between devices with their start and end apart: 5, of which 4 were waited for; matrix products, arithmetic and copies ran while one was open for 3% of the time, Pallas kernels for 0%

commit v1 on v0

--- a/solution.py
+++ b/solution.py
@@ -2,6 +2,17 @@
 import jax.numpy as jnp
 from jax import lax
 from jax.sharding import PartitionSpec as P
+
+
+def cut_along(x, dim, devices):
+    before, after = (x.shape[:dim], x.shape[dim + 1 :])
+    return jnp.moveaxis(x.reshape(*before, devices, -1, *after), dim, 0)
+
+
+def laid_out(blocks, dim):
+    blocks = jnp.moveaxis(blocks, 0, dim)
+    dims = blocks.shape
+    return blocks.reshape(*dims[:dim], dims[dim] * dims[dim + 1], *dims[dim + 2 :])
 
 
 def local(three_index, fock_diag, pair_occ, pno_count, pno_energy, pno_coef):
@@ -44,13 +55,16 @@
     proj_here = jnp.einsum(
         "sdp,sdq->spq", coef_recv, selected, preferred_element_type=jnp.float32
     ).astype(jnp.bfloat16)
-    proj_back = lax.all_to_all(
-        proj_here.reshape(groups, capacity, width_pno, width_aux),
-        "pair",
-        split_axis=0,
-        concat_axis=0,
-        tiled=True,
-    )
+    x = proj_here.reshape(groups, capacity, width_pno, width_aux)
+    size, position = (lax.axis_size("pair"), lax.axis_index("pair"))
+    tiles = cut_along(x, 0, size)
+    out = tiles
+    for lap in range(1, size):
+        target, source = ((position + lap) % size, (position - lap) % size)
+        sent = lax.dynamic_index_in_dim(tiles, target, 0)
+        partner_block = lax.ppermute(sent, "pair", [(i, (i + lap) % size) for i in range(size)])
+        out = lax.dynamic_update_slice_in_dim(out, partner_block, source, axis=0)
+    proj_back = laid_out(out, 0)
     projected = jnp.take(proj_back.reshape(slots, width_pno, width_aux), slot_of, axis=0)
     paired = projected.reshape(pair_dev, 2, width_pno, width_aux)
     rows_i = paired[:, 0]

time: 1190 us -> 1230 us (1.034)
  local copies, waits for them, and re-layouts: 131 us -> 169 us
  starting transfers between devices: 24.4 us -> 59.2 us
  waiting for transfers between devices: 859 us -> 827 us
    all_to_all x1 -> x0, waiting for transfers between devices: 361 us -> none  [local(): lax.all_to_all(proj_here.reshape(groups, capacity, width_pno, width_aux),...]
    ppermute x0 -> x15, waiting for transfers between devices: none -> 323 us  [local(): lax.ppermute(sent, 'pair', [(i, (i + lap) % size) for i in range(size)])]
    ppermute x0 -> x15, starting transfers between devices: none -> 40.1 us  [local(): lax.ppermute(sent, 'pair', [(i, (i + lap) % size) for i in range(size)])]
    dynamic_update_slice x0 -> x14, local copies, waits for them, and re-layouts: none -> 25.6 us  [local(): out = lax.dynamic_update_slice_in_dim(out, partner_block, source, axis=0)]
  transfers between devices with their start and end apart: 5 -> 19, of which waited for: 4 -> 12; matrix products, arithmetic and copies ran while one was open for 3% -> 5% of each run, Pallas kernels for 0% -> 0%
where the time goes in v1:
time: 1230 us; the launch traced here: 1220 us
  waiting for transfers between devices  827 us (67%)
  local copies, waits for them, and re-layouts  169 us (14%)
  matrix products  124 us (10%)
  starting transfers between devices  59.2 us (5%)
  other arithmetic  27.6 us (2%)
  between operations  14.7 us (1%)
    all_to_all x1, waiting for transfers between devices, local(): lax.all_to_all(gamma_send.reshape(groups, capacity, width_pno, width_aux)...  362 us
    ppermute x15, waiting for transfers between devices, local(): lax.ppermute(sent, 'pair', [(i, (i + lap) % size) for i in range(size)])  323 us
    all_to_all x1, waiting for transfers between devices, local(): lax.all_to_all(coef_send.reshape(groups, capacity, width_dom, width_pno),...  76.4 us
    psum x1, waiting for transfers between devices, local(): coupling = lax.psum(partial_sum, 'aux')  66.3 us
    dot_general x1, matrix products, local(): jnp.dot(occ_hot.astype(jnp.bfloat16), terms.reshape(slots, width_dom * wi...  60.7 us
    scatter x1, local copies, waits for them, and re-layouts, local(): jnp.zeros((slots, width_pno, width_aux), jnp.bfloat16).at[slot_of]  41.4 us
    ppermute x15, starting transfers between devices, local(): lax.ppermute(sent, 'pair', [(i, (i + lap) % size) for i in range(size)])  40.1 us
    dynamic_update_slice x14, local copies, waits for them, and re-layouts, local(): out = lax.dynamic_update_slice_in_dim(out, partner_block, source, axis=0)  25.6 us
  transfers between devices with their start and end apart: 19, of which 12 were waited for; matrix products, arithmetic and copies ran while one was open for 5% of the time, Pallas kernels for 0%

profile of v1, /device:TPU:13, one launch (start us, length us, event | category | flops | bytes accessed | tf_op | source)
XLA Modules:
  0.0 1221.2 jit_solution(6494283663696761957)
XLA Ops:
  10.0 6.5 all-to-all-start.1
  19.6 11.7 scatter_fusion
  31.3 6.4 copy.56
  37.7 6.0 all-to-all-start
  44.1 15.7 %gather_fusion = bf16[64,256,1024]{2,1,0:T(8,128)(2,1)} fusion(bf16[16,256,1024]{2,1,0:T(8,128)(2,1)} %param.8, s32[1024]{0:T(1024)S(1)} %pad_clamp_fusion.3), kind=kCustom, calls=%fused_computation.2 | custom fusion | bytes 67109120 | tf_op jit(solution)/shard_map/jit(_take)/gather | solution.py:43
  59.8 76.4 %all-to-all-done = bf16[16,4,256,128]{2,3,1,0:T(8,128)(2,1)} async-done(((bf16[16,4,256,128]{2,3,1,0:T(8,128)(2,1)}), bf16[16,4,256,128]{2,3,1,0:T(8,128)(2,1)}, u32[]{:S(2)}, u32[]{:S(2)}) %all-to-all-start) | async-done | bytes 4194336 | tf_op jit(solution)/shard_map/all_to_all | solution.py:47
  136.2 18.3 %fusion.10 = bf16[64,128,1024]{2,1,0:T(8,128)(2,1)} fusion(bf16[64,256,128]{1,2,0:T(8,128)(2,1)} %bitcast.4, bf16[64,256,1024]{2,1,0:T(8,128)(2,1)} %gather_fusion, pred[64]{0:T(512)(128)(4,1)S(1)} %broadcast_compare_fusion, pred[64]{0:T(512)(128)(4,1)S(1)} %gt.15), kind=kOutput, calls=%fused_computation.20 | convolution fusion | flops 4336910336 | bytes 54526080 | tf_op jit(solution)/shard_map/sdp,sdq->spq/dot_general | solution.py:55
  157.5 11.7 collective-permute-done
  169.2 9.5 constant_dynamic-slice_fusion
  187.3 15.2 %collective-permute-done.1 = bf16[1,1,4,128,1024]{4,3,2,0,1:T(8,128)(2,1)S(1)} collective-permute-done((bf16[1,1,4,128,1024]{4,3,2,0,1:T(8,128)(2,1)S(1)}, bf16[1,1,4,128,1024]{4,3,2,0,1:T(8,128)(2,1)S(1)}, u32[]{:S(2)}, u32[]{:S(2)}) %collective-permute-start.1) | collective-permute-done | bytes 1048608 | tf_op jit(solution)/shard_map/ppermute | solution.py:65
  207.4 12.8 %collective-permute-done.2 = bf16[1,1,4,128,1024]{4,3,2,0,1:T(8,128)(2,1)S(1)} collective-permute-done((bf16[1,1,4,128,1024]{4,3,2,0,1:T(8,128)(2,1)S(1)}, bf16[1,1,4,128,1024]{4,3,2,0,1:T(8,128)(2,1)S(1)}, u32[]{:S(2)}, u32[]{:S(2)}) %collective-permute-start.2) | collective-permute-done | bytes 1048608 | tf_op jit(solution)/shard_map/ppermute | solution.py:65
  220.2 26.9 %collective-permute-done.3 = bf16[1,1,4,128,1024]{4,3,2,0,1:T(8,128)(2,1)S(1)} collective-permute-done((bf16[1,1,4,128,1024]{4,3,2,0,1:T(8,128)(2,1)S(1)}, bf16[1,1,4,128,1024]{4,3,2,0,1:T(8,128)(2,1)S(1)}, u32[]{:S(2)}, u32[]{:S(2)}) %collective-permute-start.3) | collective-permute-done | bytes 1048608 | tf_op jit(solution)/shard_map/ppermute | solution.py:65
  247.1 152.9 %collective-permute-done.4 = bf16[1,1,4,128,1024]{4,3,2,0,1:T(8,128)(2,1)S(1)} collective-permute-done((bf16[1,1,4,128,1024]{4,3,2,0,1:T(8,128)(2,1)S(1)}, bf16[1,1,4,128,1024]{4,3,2,0,1:T(8,128)(2,1)S(1)}, u32[]{:S(2)}, u32[]{:S(2)}) %collective-permute-start.4) | collective-permute-done | bytes 1048608 | tf_op jit(solution)/shard_map/ppermute | solution.py:65
  403.8 30.0 %collective-permute-done.5 = bf16[1,1,4,128,1024]{4,3,2,0,1:T(8,128)(2,1)} collective-permute-done((bf16[1,1,4,128,1024]{4,3,2,0,1:T(8,128)(2,1)}, bf16[1,1,4,128,1024]{4,3,2,0,1:T(8,128)(2,1)}, u32[]{:S(2)}, u32[]{:S(2)}) %collective-permute-start.5) | collective-permute-done | bytes 1048608 | tf_op jit(solution)/shard_map/ppermute | solution.py:65
  436.0 31.4 %collective-permute-done.6 = bf16[1,1,4,128,1024]{4,3,2,0,1:T(8,128)(2,1)} collective-permute-done((bf16[1,1,4,128,1024]{4,3,2,0,1:T(8,128)(2,1)}, bf16[1,1,4,128,1024]{4,3,2,0,1:T(8,128)(2,1)}, u32[]{:S(2)}, u32[]{:S(2)}) %collective-permute-start.6) | collective-permute-done | bytes 1048608 | tf_op jit(solution)/shard_map/ppermute | solution.py:65
  469.7 31.4 %collective-permute-done.7 = bf16[1,1,4,128,1024]{4,3,2,0,1:T(8,128)(2,1)} collective-permute-done((bf16[1,1,4,128,1024]{4,3,2,0,1:T(8,128)(2,1)}, bf16[1,1,4,128,1024]{4,3,2,0,1:T(8,128)(2,1)}, u32[]{:S(2)}, u32[]{:S(2)}) %collective-permute-start.7) | collective-permute-done | bytes 1048608 | tf_op jit(solution)/shard_map/ppermute | solution.py:65
  505.7 24.8 %collective-permute-start.14 = (bf16[1,1,4,128,1024]{4,3,2,0,1:T(8,128)(2,1)S(1)}, bf16[1,1,4,128,1024]{4,3,2,0,1:T(8,128)(2,1)S(1)}, u32[]{:S(2)}, u32[]{:S(2)}) collective-permute-start(bf16[1,1,4,128,1024]{4,3,2,0,1:T(8,128)(2,1)S(1)} %get-tuple-element.11), channel_id=1, source_target_pairs={{0,15},{1,0},{2,1},{3,2},{4,3},{5,4},{6,5},{7,6},{8,7},{9,8},{10,9... | collective-permute-start | bytes 3145736 | tf_op jit(solution)/shard_map/ppermute | solution.py:65
  543.7 10.6 collective-permute-done.14
  555.4 13.3 %gather_fusion.1 = bf16[62,128,1024]{2,1,0:T(8,128)(2,1)} fusion(bf16[64,128,1024]{2,1,0:T(8,128)(2,1)} %bitcast.71, s32[1024]{0:T(1024)S(1)} %pad_clamp_fusion.2), kind=kCustom, calls=%fused_computation.3 | custom fusion | bytes 32506104 | tf_op jit(solution)/shard_map/jit(_take)/gather | solution.py:68
  568.6 13.9 %copy_select_fusion = bf16[31,2,128,1024]{3,2,0,1:T(8,128)(2,1)} fusion(bf16[31,2,128,1024]{3,2,1,0:T(8,128)(2,1)} %bitcast.68, pred[31,2]{0,1:T(4,128)(4,1)S(1)} %compare_and_fusion), kind=kLoop, calls=%fused_computation.19 | loop fusion | flops 8126464 | bytes 32505918 | tf_op jit(solution)/shard_map/jit(_take)/select_n | solution.py:68
  582.6 9.2 fusion.14
  593.3 66.3 %all-reduce.2.cloned.1.call-done = f32[31,128,128]{2,1,0:T(8,128)} async-done(((f32[31,128,128]{2,1,0:T(8,128)}), f32[31,128,128]{2,1,0:T(8,128)}) %all-reduce.2.cloned.1.call-update) | async-done | bytes 2031632 | tf_op jit(solution)/shard_map/psum | solution.py:73
  676.9 8.7 convert_bitcast_fusion.1
  685.6 6.2 pad_maximum_fusion
  691.8 6.5 copy.62
  698.3 6.1 broadcast_in_dim.68
  704.4 41.4 %scatter_fusion.1 = bf16[64,128,1024]{2,1,0:T(8,128)(2,1)} fusion(bf16[64,128,1024]{2,1,0:T(8,128)(2,1)} %broadcast_in_dim.68, s32[62]{0:T(128)S(1)} %fusion.25, bf16[62,128,1024]{2,1,0:T(8,128)(2,1)} %bitcast.67), kind=kCustom, calls=%fused_computation.6 | custom fusion | bytes 48759032 | tf_op jit(solution)/shard_map/scatter | solution.py:90
  745.7 6.5 all-to-all-start.2
  752.8 361.6 %all-to-all-done.2 = bf16[16,4,128,1024]{3,2,1,0:T(8,128)(2,1)} async-done(((bf16[16,4,128,1024]{3,2,1,0:T(8,128)(2,1)}), bf16[16,4,128,1024]{3,2,1,0:T(8,128)(2,1)}, u32[]{:S(2)}, u32[]{:S(2)}) %all-to-all-start.2) | async-done | bytes 16777248 | tf_op jit(solution)/shard_map/all_to_all | solution.py:91
  1114.4 21.4 %convolution_convert_fusion = bf16[64,256,1024]{2,1,0:T(8,128)(2,1)} fusion(bf16[64,256,128]{1,2,0:T(8,128)(2,1)} %bitcast.4, bf16[64,128,1024]{2,1,0:T(8,128)(2,1)} %bitcast.19), kind=kOutput, calls=%fused_computation.15 | convolution fusion | flops 4311744512 | bytes 54525952 | tf_op jit(solution)/shard_map/sdp,spq->sdq/dot_general | solution.py:99
  1135.7 60.7 %fusion = f32[16,256,1024]{2,0,1:T(8,128)} fusion(s32[64]{0:T(128)S(1)} %copy-done.9, pred[64]{0:T(512)(128)(4,1)S(1)} %gt.15, bf16[8,8,256,1024]{3,2,1,0:T(8,128)(2,1)} %bitcast.65), kind=kOutput, calls=%fused_computation.7 | convolution fusion | flops 536872960 | bytes 50331968 | tf_op jit(solution)/shard_map/dot_general | solution.py:105
  1196.5 17.8 %copy.65 = f32[16,256,1024]{2,1,0:T(8,128)} copy(f32[16,256,1024]{2,0,1:T(8,128)} %fusion) | data formatting | bytes 33554432
  (93 shorter events, 68.8 us)
Async XLA Ops:
  7.2 584.7 %copy-start = (f32[256]{0:T(256)S(1)}, f32[256]{0:T(256)}, u32[]{:S(2)}) copy-start(f32[256]{0:T(256)} %param.9) | copy-start | bytes 3076
  10.0 27.7 %all-to-all-start.1 = ((s32[16,1,4]{2,1,0:T(1,128)}), s32[16,1,4]{2,1,0:T(1,128)S(1)}, u32[]{:S(2)}, u32[]{:S(2)}) async-start(s32[16,1,4]{2,1,0:T(1,128)} %bitcast.5), calls=%async_computation.1 | async-start | bytes 16384 | tf_op jit(solution)/shard_map/all_to_all | solution.py:38
  37.7 98.5 %all-to-all-start = ((bf16[16,4,256,128]{2,3,1,0:T(8,128)(2,1)}), bf16[16,4,256,128]{2,3,1,0:T(8,128)(2,1)}, u32[]{:S(2)}, u32[]{:S(2)}) async-start(bf16[16,4,256,128]{2,3,1,0:T(8,128)(2,1)} %copy.56), calls=%async_computation | async-start | bytes 8388608 | tf_op jit(solution)/shard_map/all_to_all | solution.py:47
  43.7 615.9 %all-reduce.2.cloned.1.call-start = ((), (), s32[]{:S(2)}) async-start(), calls=%async_computation.3 | async-start | bytes 4063232 | tf_op jit(solution)/shard_map/psum | solution.py:73
  43.9 15.9 %copy-start.8 = (s32[64]{0:T(128)}, s32[64]{0:T(128)S(1)}, u32[]{:S(2)}) copy-start(s32[64]{0:T(128)S(1)} %max.23) | copy-start | bytes 772
  155.8 245.7 %copy-start.7 = (s32[31,2]{0,1:T(2,128)S(1)}, s32[31,2]{0,1:T(2,128)}, u32[]{:S(2)}) copy-start(s32[31,2]{0,1:T(2,128)} %param.10) | copy-start | bytes 748
  155.8 13.5 %collective-permute-start = (bf16[1,1,4,128,1024]{4,3,2,0,1:T(8,128)(2,1)S(1)}, bf16[1,1,4,128,1024]{4,3,2,0,1:T(8,128)(2,1)}, u32[]{:S(2)}, u32[]{:S(2)}) collective-permute-start(bf16[1,1,4,128,1024]{4,3,2,0,1:T(8,128)(2,1)S(1)} %constant_dynamic-slice_fusion.14), channel_id=1, source_target_pairs={{0,1},{1,2},{2,3},{3,4},{4,5},{5,6},{6,7},{7,8},{8,9},{9,10},{10,1... | collective-permute-start | bytes 3145736 | tf_op jit(solution)/shard_map/ppermute | solution.py:65
  178.7 23.7 %collective-permute-start.1 = (bf16[1,1,4,128,1024]{4,3,2,0,1:T(8,128)(2,1)S(1)}, bf16[1,1,4,128,1024]{4,3,2,0,1:T(8,128)(2,1)S(1)}, u32[]{:S(2)}, u32[]{:S(2)}) collective-permute-start(bf16[1,1,4,128,1024]{4,3,2,0,1:T(8,128)(2,1)S(1)} %get-tuple-element.24), channel_id=1, source_target_pairs={{0,2},{1,3},{2,4},{3,5},{4,6},{5,7},{6,8},{7,9},{8,10},{9,11},{10,... | collective-permute-start | bytes 3145736 | tf_op jit(solution)/shard_map/ppermute | solution.py:65
  178.8 41.4 %collective-permute-start.2 = (bf16[1,1,4,128,1024]{4,3,2,0,1:T(8,128)(2,1)S(1)}, bf16[1,1,4,128,1024]{4,3,2,0,1:T(8,128)(2,1)S(1)}, u32[]{:S(2)}, u32[]{:S(2)}) collective-permute-start(bf16[1,1,4,128,1024]{4,3,2,0,1:T(8,128)(2,1)S(1)} %get-tuple-element.23), channel_id=1, source_target_pairs={{0,3},{1,4},{2,5},{3,6},{4,7},{5,8},{6,9},{7,10},{8,11},{9,12},{10... | collective-permute-start | bytes 3145736 | tf_op jit(solution)/shard_map/ppermute | solution.py:65
  179.9 67.2 %collective-permute-start.3 = (bf16[1,1,4,128,1024]{4,3,2,0,1:T(8,128)(2,1)S(1)}, bf16[1,1,4,128,1024]{4,3,2,0,1:T(8,128)(2,1)S(1)}, u32[]{:S(2)}, u32[]{:S(2)}) collective-permute-start(bf16[1,1,4,128,1024]{4,3,2,0,1:T(8,128)(2,1)S(1)} %get-tuple-element.22), channel_id=1, source_target_pairs={{0,4},{1,5},{2,6},{3,7},{4,8},{5,9},{6,10},{7,11},{8,12},{9,13},{1... | collective-permute-start | bytes 3145736 | tf_op jit(solution)/shard_map/ppermute | solution.py:65
  184.1 215.8 %collective-permute-start.4 = (bf16[1,1,4,128,1024]{4,3,2,0,1:T(8,128)(2,1)S(1)}, bf16[1,1,4,128,1024]{4,3,2,0,1:T(8,128)(2,1)S(1)}, u32[]{:S(2)}, u32[]{:S(2)}) collective-permute-start(bf16[1,1,4,128,1024]{4,3,2,0,1:T(8,128)(2,1)S(1)} %get-tuple-element.21), channel_id=1, source_target_pairs={{0,5},{1,6},{2,7},{3,8},{4,9},{5,10},{6,11},{7,12},{8,13},{9,14},{... | collective-permute-start | bytes 3145736 | tf_op jit(solution)/shard_map/ppermute | solution.py:65
  184.1 249.7 %collective-permute-start.5 = (bf16[1,1,4,128,1024]{4,3,2,0,1:T(8,128)(2,1)}, bf16[1,1,4,128,1024]{4,3,2,0,1:T(8,128)(2,1)}, u32[]{:S(2)}, u32[]{:S(2)}) collective-permute-start(bf16[1,1,4,128,1024]{4,3,2,0,1:T(8,128)(2,1)} %get-tuple-element.20), channel_id=1, source_target_pairs={{0,6},{1,7},{2,8},{3,9},{4,10},{5,11},{6,12},{7,13},{8,14},{9,15},... | collective-permute-start | bytes 3145736 | tf_op jit(solution)/shard_map/ppermute | solution.py:65
  202.5 198.5 %copy-start.5 = (bf16[1,1,4,128,1024]{4,3,2,0,1:T(8,128)(2,1)}, bf16[1,1,4,128,1024]{4,3,2,0,1:T(8,128)(2,1)S(1)}, u32[]{:S(2)}) copy-start(bf16[1,1,4,128,1024]{4,3,2,0,1:T(8,128)(2,1)S(1)} %collective-permute-done.1) | copy-start | bytes 3145732
  202.5 265.0 %collective-permute-start.6 = (bf16[1,1,4,128,1024]{4,3,2,0,1:T(8,128)(2,1)}, bf16[1,1,4,128,1024]{4,3,2,0,1:T(8,128)(2,1)}, u32[]{:S(2)}, u32[]{:S(2)}) collective-permute-start(bf16[1,1,4,128,1024]{4,3,2,0,1:T(8,128)(2,1)} %get-tuple-element.19), channel_id=1, source_target_pairs={{0,7},{1,8},{2,9},{3,10},{4,11},{5,12},{6,13},{7,14},{8,15},{9,0},... | collective-permute-start | bytes 3145736 | tf_op jit(solution)/shard_map/ppermute | solution.py:65
  220.2 180.8 %copy-start.4 = (bf16[1,1,4,128,1024]{4,3,2,0,1:T(8,128)(2,1)}, bf16[1,1,4,128,1024]{4,3,2,0,1:T(8,128)(2,1)S(1)}, u32[]{:S(2)}) copy-start(bf16[1,1,4,128,1024]{4,3,2,0,1:T(8,128)(2,1)S(1)} %collective-permute-done.2) | copy-start | bytes 3145732
  220.2 281.0 %collective-permute-start.7 = (bf16[1,1,4,128,1024]{4,3,2,0,1:T(8,128)(2,1)}, bf16[1,1,4,128,1024]{4,3,2,0,1:T(8,128)(2,1)}, u32[]{:S(2)}, u32[]{:S(2)}) collective-permute-start(bf16[1,1,4,128,1024]{4,3,2,0,1:T(8,128)(2,1)} %get-tuple-element.18), channel_id=1, source_target_pairs={{0,8},{1,9},{2,10},{3,11},{4,12},{5,13},{6,14},{7,15},{8,0},{9,1},... | collective-permute-start | bytes 3145736 | tf_op jit(solution)/shard_map/ppermute | solution.py:65
  247.0 153.9 %copy-start.3 = (bf16[1,1,4,128,1024]{4,3,2,0,1:T(8,128)(2,1)}, bf16[1,1,4,128,1024]{4,3,2,0,1:T(8,128)(2,1)S(1)}, u32[]{:S(2)}) copy-start(bf16[1,1,4,128,1024]{4,3,2,0,1:T(8,128)(2,1)S(1)} %collective-permute-done.3) | copy-start | bytes 3145732
  247.0 256.4 %collective-permute-start.8 = (bf16[1,1,4,128,1024]{4,3,2,0,1:T(8,128)(2,1)}, bf16[1,1,4,128,1024]{4,3,2,0,1:T(8,128)(2,1)}, u32[]{:S(2)}, u32[]{:S(2)}) collective-permute-start(bf16[1,1,4,128,1024]{4,3,2,0,1:T(8,128)(2,1)} %get-tuple-element.17), channel_id=1, source_target_pairs={{0,9},{1,10},{2,11},{3,12},{4,13},{5,14},{6,15},{7,0},{8,1},{9,2},... | collective-permute-start | bytes 3145736 | tf_op jit(solution)/shard_map/ppermute | solution.py:65
  399.9 1.0 copy-start.2
  400.9 104.8 %collective-permute-start.9 = (bf16[1,1,4,128,1024]{4,3,2,0,1:T(8,128)(2,1)}, bf16[1,1,4,128,1024]{4,3,2,0,1:T(8,128)(2,1)}, u32[]{:S(2)}, u32[]{:S(2)}) collective-permute-start(bf16[1,1,4,128,1024]{4,3,2,0,1:T(8,128)(2,1)} %get-tuple-element.16), channel_id=1, source_target_pairs={{0,10},{1,11},{2,12},{3,13},{4,14},{5,15},{6,0},{7,1},{8,2},{9,3},... | collective-permute-start | bytes 3145736 | tf_op jit(solution)/shard_map/ppermute | solution.py:65
  433.8 105.8 %collective-permute-start.10 = (bf16[1,1,4,128,1024]{4,3,2,0,1:T(8,128)(2,1)}, bf16[1,1,4,128,1024]{4,3,2,0,1:T(8,128)(2,1)S(1)}, u32[]{:S(2)}, u32[]{:S(2)}) collective-permute-start(bf16[1,1,4,128,1024]{4,3,2,0,1:T(8,128)(2,1)} %get-tuple-element.15), channel_id=1, source_target_pairs={{0,11},{1,12},{2,13},{3,14},{4,15},{5,0},{6,1},{7,2},{8,3},{9,4},{... | collective-permute-start | bytes 3145736 | tf_op jit(solution)/shard_map/ppermute | solution.py:65
  467.5 73.1 %collective-permute-start.11 = (bf16[1,1,4,128,1024]{4,3,2,0,1:T(8,128)(2,1)}, bf16[1,1,4,128,1024]{4,3,2,0,1:T(8,128)(2,1)S(1)}, u32[]{:S(2)}, u32[]{:S(2)}) collective-permute-start(bf16[1,1,4,128,1024]{4,3,2,0,1:T(8,128)(2,1)} %get-tuple-element.14), channel_id=1, source_target_pairs={{0,12},{1,13},{2,14},{3,15},{4,0},{5,1},{6,2},{7,3},{8,4},{9,5},{1... | collective-permute-start | bytes 3145736 | tf_op jit(solution)/shard_map/ppermute | solution.py:65
  501.2 40.5 %collective-permute-start.12 = (bf16[1,1,4,128,1024]{4,3,2,0,1:T(8,128)(2,1)S(1)}, bf16[1,1,4,128,1024]{4,3,2,0,1:T(8,128)(2,1)S(1)}, u32[]{:S(2)}, u32[]{:S(2)}) collective-permute-start(bf16[1,1,4,128,1024]{4,3,2,0,1:T(8,128)(2,1)S(1)} %get-tuple-element.13), channel_id=1, source_target_pairs={{0,13},{1,14},{2,15},{3,0},{4,1},{5,2},{6,3},{7,4},{8,5},{9,6},{10... | collective-permute-start | bytes 3145736 | tf_op jit(solution)/shard_map/ppermute | solution.py:65
  503.4 39.2 %collective-permute-start.13 = (bf16[1,1,4,128,1024]{4,3,2,0,1:T(8,128)(2,1)S(1)}, bf16[1,1,4,128,1024]{4,3,2,0,1:T(8,128)(2,1)S(1)}, u32[]{:S(2)}, u32[]{:S(2)}) collective-permute-start(bf16[1,1,4,128,1024]{4,3,2,0,1:T(8,128)(2,1)S(1)} %get-tuple-element.12), channel_id=1, source_target_pairs={{0,14},{1,15},{2,0},{3,1},{4,2},{5,3},{6,4},{7,5},{8,6},{9,7},{10,... | collective-permute-start | bytes 3145736 | tf_op jit(solution)/shard_map/ppermute | solution.py:65
  505.7 48.6 %collective-permute-start.14 = (bf16[1,1,4,128,1024]{4,3,2,0,1:T(8,128)(2,1)S(1)}, bf16[1,1,4,128,1024]{4,3,2,0,1:T(8,128)(2,1)S(1)}, u32[]{:S(2)}, u32[]{:S(2)}) collective-permute-start(bf16[1,1,4,128,1024]{4,3,2,0,1:T(8,128)(2,1)S(1)} %get-tuple-element.11), channel_id=1, source_target_pairs={{0,15},{1,0},{2,1},{3,2},{4,3},{5,4},{6,5},{7,6},{8,7},{9,8},{10,9... | collective-permute-start | bytes 3145736 | tf_op jit(solution)/shard_map/ppermute | solution.py:65
  582.6 10.7 copy-start.10
  582.6 79.4 %copy-start.6 = (f32[31,128]{1,0:T(8,128)S(1)}, f32[31,128]{1,0:T(8,128)}, u32[]{:S(2)}) copy-start(f32[31,128]{1,0:T(8,128)} %param.12) | copy-start | bytes 47620
  745.7 368.6 %all-to-all-start.2 = ((bf16[16,4,128,1024]{3,2,1,0:T(8,128)(2,1)}), bf16[16,4,128,1024]{3,2,1,0:T(8,128)(2,1)}, u32[]{:S(2)}, u32[]{:S(2)}) async-start(bf16[16,4,128,1024]{3,2,1,0:T(8,128)(2,1)} %bitcast.66), calls=%async_computation.2 | async-start | bytes 33554432 | tf_op jit(solution)/shard_map/all_to_all | solution.py:91
  1114.4 21.4 %copy-start.9 = (s32[64]{0:T(128)S(1)}, s32[64]{0:T(128)}, u32[]{:S(2)}) copy-start(s32[64]{0:T(128)} %copy-done.8) | copy-start | bytes 772
  1135.7 78.5 %copy-start.1 = (f32[256]{0:T(256)S(1)}, f32[256]{0:T(256)}, u32[]{:S(2)}) copy-start(f32[256]{0:T(256)} %param.9) | copy-start | bytes 3076
Sparse Core Ops, SparseCore 0:
  591.9 67.6 all-reduce.1
